TPU v7x, 256 devices: a whole 4x4x8 slice. The times are simulated.
256 devices in a mesh: gx: 32 (over y_lo, z, core), gy: 8 (over y_hi, x).
Axes of the slice: x: 4, y: 4 (y_hi: 2, y_lo: 2; y = y_hi * 2 + y_lo), z: 8, core: 2. Of those that a mesh axis runs over, the one named last changes fastest.
Arguments:
- fields: float32 [5, 1, 4096, 4096], P(None, None, 'gx', 'gy'), may hold values from -5 to 5
- metric_x: float32 [4096], P('gx'), may hold values from 0.5 to 2
- metric_y: float32 [4096], P('gy'), may hold values from 0.5 to 2
Outputs:
- first_x: float32 [5, 1, 4096, 4096], P(None, None, 'gx', 'gy')
- second_x: float32 [5, 1, 4096, 4096], P(None, None, 'gx', 'gy')
- first_y: float32 [5, 1, 4096, 4096], P(None, None, 'gx', 'gy')
- second_y: float32 [5, 1, 4096, 4096], P(None, None, 'gx', 'gy')
All inputs are finite; a program needn't handle non-finite values.
Results may differ from a plain program's by a relative error of at most 0.0001.
Values sent between devices are 32-bit elements; how exact they have to be, the bound alone decides.
A program may use at most 128 MiB of HBM per device.

v0:
```python
import functools

import jax
import jax.numpy as jnp
import numpy as np
from jax import lax
from jax.experimental import pallas as pl
from jax.experimental.pallas import tpu as pltpu
from jax.sharding import PartitionSpec as P

MESH = pl.DeviceIdType.MESH
F32 = jnp.float32
BF16 = jnp.bfloat16

ALPHA = (1.0 / 3.0, 2.0 / 11.0)
NEAR = (7.0 / 9.0, 12.0 / 11.0 + 6.0 / 44.0)
FAR = (1.0 / 36.0, 3.0 / 44.0)
RHO = tuple(-(1.0 - np.sqrt(1.0 - 4.0 * a * a)) / (2.0 * a) for a in ALPHA)
GAIN = tuple(1.0 / np.sqrt(1.0 - 4.0 * a * a) for a in ALPHA)


def flushed(table):
    table = np.asarray(table, np.float64)
    return np.where(np.abs(table) < np.finfo(np.float32).tiny, 0.0, table)


def halves(table):
    table = flushed(table).astype(np.float32)
    high = table.astype(jnp.bfloat16)
    low = (table - high.astype(np.float32)).astype(jnp.bfloat16)
    return high, low


def green(distance, which):
    return GAIN[which] * np.power(RHO[which], np.abs(distance))


def line_tables(count):
    cells = np.arange(count)
    out = [halves(green(cells[:, None] - cells[None, :], w)) for w in range(2)]
    return np.stack([np.stack(pair) for pair in out])


def window_tables():
    rows = np.arange(512)[:, None]
    cols = np.arange(256)[None, :]
    out = [halves(green(rows - 128 - cols, w)) for w in range(2)]
    return np.stack([np.stack(pair) for pair in out])


def edge_rows(count):
    cells = np.arange(count)
    out = np.zeros((24, count))
    for w in range(2):
        out[2 * w] = green(count - 1 - cells, w)
        out[2 * w + 1] = green(cells, w)
        out[8 + 2 * w : 10 + 2 * w] = NEAR[w]
        out[16 + 2 * w : 18 + 2 * w] = FAR[w]
    return flushed(out).astype(np.float32)


def face_columns(count, which):
    cells = np.arange(count)
    out = np.zeros((count, 4))
    rho, fix = RHO[which], GAIN[which] * (RHO[which] - 1.0 / RHO[which])
    out[:, 0] = np.power(rho, cells)
    out[0, 1] = fix
    out[:, 2] = np.power(rho, count - 1 - cells)
    out[count - 1, 3] = fix
    return out


def face_tables_x(fields, count):
    tables = np.zeros((2, fields * count, 128), jnp.bfloat16)
    for w in range(2):
        high, low = halves(face_columns(count, w))
        for k in range(fields):
            for v in range(4):
                rows = slice(k * count, (k + 1) * count)
                tables[w, rows, 8 * v + k] = high[:, v]
                tables[w, rows, 32 + 8 * v + k] = low[:, v]
                tables[w, rows, 64 + 8 * v + k] = high[:, v]
    return tables


def face_tables_y(count):
    tables = np.zeros((256, 4 * count), jnp.bfloat16)
    for w in range(2):
        high, low = halves(face_columns(count, w))
        for v in range(4):
            cols = slice((2 * w + v // 2) * count, (2 * w + v // 2 + 1) * count)
            row = 32 * w + 8 * v
            tables[row, cols] = high[:, v]
            tables[64 + row, cols] = high[:, v]
            tables[128 + row, cols] = low[:, v]
    return tables


def split(value):
    high = value.astype(BF16)
    return high, (value - high.astype(F32)).astype(BF16)


def dot(a, b):
    return jnp.dot(a, b, preferred_element_type=F32)


def right_sides(f, scale, along):
    count = f.shape[along]
    place = lax.broadcasted_iota(jnp.int32, f.shape, along)
    inside = (place > 0) & (place < count - 1)
    after = pltpu.roll(f, count - 1, along)
    before = pltpu.roll(f, 1, along)
    d = jnp.where(inside, after - before, 0.0)
    e = jnp.where(inside, (after - (f + f)) + before, 0.0)
    out = []
    for which, value in ((0, d), (1, e)):
        weight = scale if which == 0 else scale * scale
        sides = pltpu.roll(value, count - 1, along) + pltpu.roll(value, 1, along)
        out.append(weight * (NEAR[which] * value + FAR[which] * sides))
    return out


def edge_weights(table, metric):
    count = metric.shape[1]
    row = lax.broadcasted_iota(jnp.int32, (8, count), 0)
    lane = lax.broadcasted_iota(jnp.int32, (8, count), 1)
    m = jnp.broadcast_to(metric, (8, count))
    base = table[0:8] * jnp.where(row < 2, m, m * m)
    out = table[8:16] * base + table[16:24] * (pltpu.roll(base, 1, 1) + pltpu.roll(base, count - 1, 1))
    return jnp.where((lane > 0) & (lane < count - 1), out, 0.0)


def exchange(
    nx, ny, f_hbm, mx_hbm, my_hbm, edge_hbm, tx_hbm, ty_hbm,
    ux1, ux2, uy1, uy2, sx, sy, hx, hy,
    f, mx, my, edge, tx, ty, pack, column, load, send, recv,
):
    fields, rows, cols = f.shape
    ix, iy = lax.axis_index("gx"), lax.axis_index("gy")
    peers = (
        {"gx": lax.rem(ix + 1, nx)},
        {"gx": lax.rem(ix + nx - 1, nx)},
        {"gy": lax.rem(iy + 1, ny)},
        {"gy": lax.rem(iy + ny - 1, ny)},
    )
    barrier = pltpu.get_barrier_semaphore()
    for peer in peers:
        pl.semaphore_signal(barrier, inc=1, device_id=peer, device_id_type=MESH)
    loads = [
        pltpu.make_async_copy(mx_hbm, mx, load.at[0]),
        pltpu.make_async_copy(my_hbm, my, load.at[1]),
        pltpu.make_async_copy(edge_hbm, edge, load.at[2]),
    ]
    loads += [pltpu.make_async_copy(f_hbm.at[k, 0], f.at[k], load.at[5 + k]) for k in range(fields)]
    loads += [pltpu.make_async_copy(tx_hbm, tx, load.at[3]), pltpu.make_async_copy(ty_hbm, ty, load.at[4])]
    for copy in loads:
        copy.start()

    lane = lax.broadcasted_iota(jnp.int32, (rows, 128), 1)
    for copy in loads[:3]:
        copy.wait()
    table = edge[...]
    scale_x = mx[...]
    along_x = jnp.broadcast_to(scale_x, (rows, rows)).T
    weights_x = edge_weights(table, scale_x)
    weights_x = jnp.concatenate([weights_x, jnp.zeros((rows - 8, rows), F32)], axis=0).T
    last1, first1, last2, first2 = (
        jnp.broadcast_to(weights_x[:, n : n + 1], (rows, 128)) for n in range(4)
    )
    for n, value in enumerate((last1, first1, last2, first2)):
        column[n] = value
    column[4] = along_x
    right_block, left_block = my[:, cols - 128 : cols], my[:, 0:128]
    weights_r = edge_weights(table, right_block)
    weights_l = edge_weights(table, left_block)

    for side in range(2):
        sx[side] = jnp.zeros((32, cols), F32)
    metric_row = jnp.broadcast_to(
        jnp.concatenate([along_x[0:2], along_x[rows - 2 : rows]], axis=0)[:, 0:1], (4, cols)
    )
    sx[0, 5:6, :] = metric_row[2:3]
    sx[0, 13:14, :] = metric_row[3:4]
    sx[1, 5:6, :] = metric_row[0:1]
    sx[1, 13:14, :] = metric_row[1:2]

    def place(tile, spot, value):
        return jnp.where(lane == spot, jnp.broadcast_to(value, tile.shape), tile)

    tile = jnp.zeros((rows, 128), F32)
    tile = place(tile, 5, right_block[:, 126:127])
    tile = place(tile, 13, right_block[:, 127:128])
    tile = place(tile, 37, left_block[:, 0:1])
    tile = place(tile, 45, left_block[:, 1:2])
    pack[...] = tile

    wide = [jnp.concatenate([column[n]] * (cols // 128), axis=1) for n in range(4)]
    for k in range(fields):
        loads[3 + k].wait()
        value = f[k]
        after, before = pltpu.roll(value, rows - 1, 0), pltpu.roll(value, 1, 0)
        d = after - before
        e = (after - (value + value)) + before
        sx[0, k : k + 1, :] = value[rows - 2 : rows - 1]
        sx[0, 8 + k : 9 + k, :] = value[rows - 1 : rows]
        sx[1, k : k + 1, :] = value[0:1]
        sx[1, 8 + k : 9 + k, :] = value[1:2]
        sx[0, 16 + k : 17 + k, :] = jnp.sum(d * wide[0], axis=0, keepdims=True)
        sx[1, 16 + k : 17 + k, :] = jnp.sum(d * wide[1], axis=0, keepdims=True)
        sx[0, 24 + k : 25 + k, :] = jnp.sum(e * wide[2], axis=0, keepdims=True)
        sx[1, 24 + k : 25 + k, :] = jnp.sum(e * wide[3], axis=0, keepdims=True)

        tile = pack[...]
        for side in range(2):
            block = value[:, cols - 128 : cols] if side == 0 else value[:, 0:128]
            weights = weights_r if side == 0 else weights_l
            after, before = pltpu.roll(block, 127, 1), pltpu.roll(block, 1, 1)
            d = after - before
            e = (after - (block + block)) + before
            near = 126 if side == 0 else 0
            tile = place(tile, 32 * side + k, block[:, near : near + 1])
            tile = place(tile, 32 * side + 8 + k, block[:, near + 1 : near + 2])
            one = jnp.sum(d * weights[side : side + 1], axis=1, keepdims=True)
            two = jnp.sum(e * weights[2 + side : 3 + side], axis=1, keepdims=True)
            tile = place(tile, 32 * side + 16 + k, one)
            tile = place(tile, 32 * side + 24 + k, two)
        pack[...] = tile

    turned = pack[...].T
    sy[0] = turned[0:32]
    sy[1] = turned[32:64]
    pl.semaphore_wait(barrier, 4)
    copies = []
    for n, peer in enumerate(peers):
        source, target = (sx, hx) if n < 2 else (sy, hy)
        copy = pltpu.make_async_remote_copy(
            src_ref=source.at[n % 2],
            dst_ref=target.at[n % 2],
            send_sem=send.at[n],
            recv_sem=recv.at[n],
            device_id=peer,
            device_id_type=MESH,
        )
        copy.start()
        copies.append(copy)

    loads[3 + fields].wait()
    loads[4 + fields].wait()
    scale_x = jnp.concatenate([column[4]] * (cols // 128), axis=1)
    scale_y = jnp.broadcast_to(my[...], (rows, cols))

    def solve(k, carry):
        value = f[k]
        for which, (right, out) in enumerate(zip(right_sides(value, scale_x, 0), (ux1, ux2))):
            high, low = split(right)
            out[k] = dot(tx[which, 0], high) + dot(tx[which, 0], low) + dot(tx[which, 1], high)
        for which, (right, out) in enumerate(zip(right_sides(value, scale_y, 1), (uy1, uy2))):
            high, low = split(right)
            for half in range(2):
                window = slice(128 * half, 128 * half + 384)
                part = slice(128 - 128 * half, 512 - 128 * half)
                out[k, :, 256 * half : 256 * half + 256] = (
                    dot(high[:, window], ty[which, 0, part])
                    + dot(low[:, window], ty[which, 0, part])
                    + dot(high[:, window], ty[which, 1, part])
                )
        return carry

    lax.fori_loop(0, fields, solve, 0)
    for copy in copies:
        copy.wait()


def face_values(own, far, side):
    near = own[1 - side]
    a, b = near[0:8], near[8:16]
    inner0, inner1 = (a, b) if side == 0 else (b, a)
    metric0, metric1 = (near[5:6], near[13:14]) if side == 0 else (near[13:14], near[5:6])
    there = far[side]
    a, b = there[0:8], there[8:16]
    outer1, outer2 = (b, a) if side == 0 else (a, b)
    beyond1, beyond2 = (there[13:14], there[5:6]) if side == 0 else (there[5:6], there[13:14])
    sign = 1.0 if side == 0 else -1.0
    differences = (
        (sign * (inner0 - outer2), sign * (inner1 - outer1)),
        ((inner0 - (outer1 + outer1)) + outer2, (inner1 - (inner0 + inner0)) + outer1),
    )
    out = []
    for which, (over, here) in enumerate(differences):
        near_by, far_by, rho, gain = NEAR[which], FAR[which], RHO[which], GAIN[which]
        m0, m1, b1, b2 = (
            (metric0, metric1, beyond1, beyond2)
            if which == 0
            else (metric0 * metric0, metric1 * metric1, beyond1 * beyond1, beyond2 * beyond2)
        )
        carry = there[16 + 8 * which : 24 + 8 * which]
        carry = carry + gain * (rho * far_by * (b2 * over) + b1 * (near_by * over + far_by * here))
        zero = m0 * (near_by * here + far_by * over)
        one = (far_by * m1) * here
        out.append((rho * carry + gain * zero + (gain / rho) * one, one))
    return out


def join(
    ux1, ux2, uy1, uy2, sx, sy, hx, hy, cx, cy,
    ox1, ox2, oy1, oy2, stage_x, stage_y, done,
):
    fields, rows, cols = ux1.shape
    middle = slice(128, cols - 128)
    copies = []

    def put(source, target):
        copy = pltpu.make_async_copy(source, target, done.at[len(copies)])
        copy.start()
        copies.append(copy)

    for part, out in ((uy1, oy1), (uy2, oy2)):
        for k in range(fields):
            put(part.at[k, :, middle], out.at[k, 0, :, middle])

    own, far = (sx[0], sx[1]), (hx[0], hx[1])
    left, right = face_values(own, far, 0), face_values(own, far, 1)
    for which, (part, out) in enumerate(((ux1, ox1), (ux2, ox2))):
        high, low = split(jnp.concatenate([*left[which], *right[which]], axis=0))
        stack = jnp.concatenate([high, high, low], axis=0)
        for k in range(fields):
            lhs = cx[which, rows * k : rows * (k + 1), 0:96]
            stage_x[which, k] = part[k] + dot(lhs, stack)
            put(stage_x.at[which, k], out.at[k, 0])

    own, far = (sy[0], sy[1]), (hy[0], hy[1])
    left, right = face_values(own, far, 0), face_values(own, far, 1)
    values = jnp.concatenate([*left[0], *right[0], *left[1], *right[1]], axis=0)
    high = values.astype(BF16).astype(F32)
    turned = jnp.concatenate([high, values - high], axis=0).T
    for k in range(fields):
        lhs = (turned if k == 0 else pltpu.roll(turned, 128 - k, 1)).astype(BF16)
        both = dot(jnp.concatenate([lhs, lhs], axis=1), cy[...])
        for which, (part, out) in enumerate(((uy1, oy1), (uy2, oy2))):
            for side in range(2):
                place = slice(0, 128) if side == 0 else slice(cols - 128, cols)
                n = 2 * which + side
                stage_y[n, k] = part[k, :, place] + both[:, 128 * n : 128 * n + 128]
                put(stage_y.at[n, k], out.at[k, 0, :, place])
    for copy in copies:
        copy.wait()


def on_device(fields, metric_x, metric_y):
    count, _, rows, cols = fields.shape
    hbm = pl.BlockSpec(memory_space=pltpu.HBM)
    vmem = pl.BlockSpec(memory_space=pltpu.VMEM)
    block = pltpu.VMEM((count, rows, cols), F32)
    parts = pl.pallas_call(
        functools.partial(exchange, lax.axis_size("gx"), lax.axis_size("gy")),
        in_specs=[hbm] * 6,
        out_specs=[vmem] * 8,
        out_shape=[
            *[block] * 4,
            pltpu.VMEM((2, 32, cols), F32),
            pltpu.VMEM((2, 32, rows), F32),
            pltpu.VMEM((2, 32, cols), F32),
            pltpu.VMEM((2, 32, rows), F32),
        ],
        scratch_shapes=[
            pltpu.VMEM((count, rows, cols), F32),
            pltpu.VMEM((1, rows), F32),
            pltpu.VMEM((1, cols), F32),
            pltpu.VMEM((24, 128), F32),
            pltpu.VMEM((2, 2, rows, rows), BF16),
            pltpu.VMEM((2, 2, 512, 256), BF16),
            pltpu.VMEM((rows, 128), F32),
            pltpu.VMEM((5, rows, 128), F32),
            pltpu.SemaphoreType.DMA((5 + count,)),
            pltpu.SemaphoreType.DMA((4,)),
            pltpu.SemaphoreType.DMA((4,)),
        ],
        compiler_params=pltpu.CompilerParams(collective_id=0, has_side_effects=True, vmem_limit_bytes=20 << 20),
        name="exchange",
    )(
        *(
            pltpu.with_memory_space_constraint(value, pltpu.HBM)
            for value in (
                fields,
                metric_x.reshape(1, rows),
                metric_y.reshape(1, cols),
                jnp.asarray(edge_rows(128)),
                jnp.asarray(line_tables(rows)),
                jnp.asarray(window_tables()),
            )
        )
    )
    return pl.pallas_call(
        join,
        in_specs=[vmem] * 10,
        out_specs=[hbm] * 4,
        out_shape=[jax.ShapeDtypeStruct(fields.shape, F32)] * 4,
        scratch_shapes=[
            pltpu.VMEM((2, count, rows, cols), F32),
            pltpu.VMEM((4, count, rows, 128), F32),
            pltpu.SemaphoreType.DMA((8 * count,)),
        ],
        compiler_params=pltpu.CompilerParams(vmem_limit_bytes=20 << 20),
        name="join",
    )(*parts, jnp.asarray(face_tables_x(count, rows)), jnp.asarray(face_tables_y(128)))


def solution(mesh):
    whole = P(None, None, "gx", "gy")
    return jax.shard_map(
        on_device,
        mesh=mesh,
        in_specs=(whole, P("gx"), P("gy")),
        out_specs=(whole,) * 4,
        check_vma=False,
    )
```

profile of v0, /device:TPU:8, one launch (start us, length us, event | category | flops | bytes accessed | tf_op | source)
XLA Modules:
  0.0 15.9 jit_solution(8013400962179405784)
XLA Ops:
  0.6 0.0 copy-start.1
  0.6 0.0 copy-start
  0.7 12.6 %exchange.1 = (f32[5,128,512]{2,1,0:T(8,128)S(1)}, f32[5,128,512]{2,1,0:T(8,128)S(1)}, f32[5,128,512]{2,1,0:T(8,128)S(1)}, f32[5,128,512]{2,1,0:T(8,128)S(1)}, f...) custom-call(f32[5,1,128,512]{3,2,1,0:T(8,128)} %f_hbm.1, ...), custom_call_target="tpu_custom_call" | custom-call | tf_op jit(solution)/shard_map/exchange/pallas_call | solution.py:355
  13.2 0.0 copy-done.1
  13.3 0.0 copy-done
  13.3 2.7 %join.1 = (f32[5,1,128,512]{3,2,1,0:T(8,128)}, f32[5,1,128,512]{3,2,1,0:T(8,128)}, f32[5,1,128,512]{3,2,1,0:T(8,128)}, f32[5,1,128,512]{3,2,1,0:T(8,128)}) custom-call(f32[5,128,512]{2,1,0:T(8,128)S(1)} %get-tuple-element.12.ux1, f32[5,128,512]{2,1,0:T(8,128)S(1)} %get-tuple-element.13.ux2, f32[5,128,512]{2,1,0:T(8,128)S(1)} %get-tuple-element.14.uy1, ...), custom_call_target="tpu_custom_call" | custom-call | tf_op jit(solution)/shard_map/join/pallas_call | solution.py:394
Async XLA Ops:
  0.6 12.6 %copy-start.1 = (bf16[256,512]{1,0:T(8,128)(2,1)S(1)}, bf16[256,512]{1,0:T(8,128)(2,1)}, u32[]{:S(2)}) copy-start(bf16[256,512]{1,0:T(8,128)(2,1)} %constant.14.clone.cy) | copy-start | bytes 786436
  0.6 12.6 %copy-start = (bf16[2,640,128]{2,1,0:T(8,128)(2,1)S(1)}, bf16[2,640,128]{2,1,0:T(8,128)(2,1)}, u32[]{:S(2)}) copy-start(bf16[2,640,128]{2,1,0:T(8,128)(2,1)} %constant.13.clone.cx) | copy-start | bytes 983044
where the time goes:
time: 16 us; the launch traced here: 15.9 us
  Pallas kernels  15.3 us (96%)
  between operations  0.67 us (4%)
    pallas_call x1, Pallas kernels, on_device(): pl.pallas_call(functools.partial(exchange, lax.axis_size('gx'), lax.axis_...  12.6 us
    pallas_call x1, Pallas kernels, on_device(): pl.pallas_call(join, in_specs=[vmem] * 10, out_specs=[hbm] * 4, out_shape...  2.67 us

commit v1 on v0

--- a/solution.py
+++ b/solution.py
@@ -11,6 +11,8 @@
 MESH = pl.DeviceIdType.MESH
 F32 = jnp.float32
 BF16 = jnp.bfloat16
+TURN, TURN_FIRST, TURN_LAST, TURN_END, TURN_SEAM = 1, 3, 0, 2, 4
+TABLES = 0
 
 ALPHA = (1.0 / 3.0, 2.0 / 11.0)
 NEAR = (7.0 / 9.0, 12.0 / 11.0 + 6.0 / 44.0)
@@ -52,10 +54,10 @@
     cells = np.arange(count)
     out = np.zeros((24, count))
     for w in range(2):
-        out[2 * w] = green(count - 1 - cells, w)
-        out[2 * w + 1] = green(cells, w)
-        out[8 + 2 * w : 10 + 2 * w] = NEAR[w]
-        out[16 + 2 * w : 18 + 2 * w] = FAR[w]
+        out[w] = green(count - 1 - cells, w)
+        out[2 + w] = green(cells, w)
+        out[8 + w : 12 + w : 2] = NEAR[w]
+        out[16 + w : 20 + w : 2] = FAR[w]
     return flushed(out).astype(np.float32)
 
 
@@ -126,15 +128,17 @@
     row = lax.broadcasted_iota(jnp.int32, (8, count), 0)
     lane = lax.broadcasted_iota(jnp.int32, (8, count), 1)
     m = jnp.broadcast_to(metric, (8, count))
-    base = table[0:8] * jnp.where(row < 2, m, m * m)
+    base = table[0:8] * jnp.where(row % 2 == 0, m, m * m)
     out = table[8:16] * base + table[16:24] * (pltpu.roll(base, 1, 1) + pltpu.roll(base, count - 1, 1))
-    return jnp.where((lane > 0) & (lane < count - 1), out, 0.0)
+    out = jnp.where((lane > 0) & (lane < count - 1), out, 0.0)
+    before, after = pltpu.roll(out, 1, 1), pltpu.roll(out, count - 1, 1)
+    return jnp.where(row % 2 == 0, before - after, (before - out) + (after - out))
 
 
 def exchange(
     nx, ny, f_hbm, mx_hbm, my_hbm, edge_hbm, tx_hbm, ty_hbm,
     ux1, ux2, uy1, uy2, sx, sy, hx, hy,
-    f, mx, my, edge, tx, ty, pack, column, load, send, recv,
+    f, mx, my, edge, tx, ty, column, load, send, recv, answer,
 ):
     fields, rows, cols = f.shape
     ix, iy = lax.axis_index("gx"), lax.axis_index("gy")
@@ -144,9 +148,33 @@
         {"gy": lax.rem(iy + 1, ny)},
         {"gy": lax.rem(iy + ny - 1, ny)},
     )
+    run = nx // 2
+    place = lax.rem(ix, run)
+    end, proxy, seam = place == run - 1, place == run - 2, place == 0
+    inner = jnp.logical_not(end)
+    right, left, up, down = peers
     barrier = pltpu.get_barrier_semaphore()
-    for peer in peers:
+
+    def greet(peer):
         pl.semaphore_signal(barrier, inc=1, device_id=peer, device_id_type=MESH)
+
+    greet(left)
+
+    @pl.when(inner)
+    def _():
+        greet(up)
+        greet(down)
+
+    @pl.when(jnp.logical_not(end | proxy))
+    def _():
+        greet(right)
+
+    @pl.when(end)
+    def _():
+        greet({**left, **up})
+        greet({**left, **down})
+
+    greeted = jnp.where(end, 1, jnp.where(proxy, 6, jnp.where(seam, 3, 4)))
     loads = [
         pltpu.make_async_copy(mx_hbm, mx, load.at[0]),
         pltpu.make_async_copy(my_hbm, my, load.at[1]),
@@ -154,100 +182,91 @@
     ]
     loads += [pltpu.make_async_copy(f_hbm.at[k, 0], f.at[k], load.at[5 + k]) for k in range(fields)]
     loads += [pltpu.make_async_copy(tx_hbm, tx, load.at[3]), pltpu.make_async_copy(ty_hbm, ty, load.at[4])]
-    for copy in loads:
+    for copy in loads[: 3 + fields]:
         copy.start()
 
-    lane = lax.broadcasted_iota(jnp.int32, (rows, 128), 1)
+    @pl.when(end)
+    def _():
+        pl.semaphore_wait(barrier, greeted)
+        pl.semaphore_signal(answer.at[0], inc=1, device_id=right, device_id_type=MESH)
+
     for copy in loads[:3]:
         copy.wait()
     table = edge[...]
     scale_x = mx[...]
-    along_x = jnp.broadcast_to(scale_x, (rows, rows)).T
-    weights_x = edge_weights(table, scale_x)
-    weights_x = jnp.concatenate([weights_x, jnp.zeros((rows - 8, rows), F32)], axis=0).T
-    last1, first1, last2, first2 = (
-        jnp.broadcast_to(weights_x[:, n : n + 1], (rows, 128)) for n in range(4)
-    )
-    for n, value in enumerate((last1, first1, last2, first2)):
-        column[n] = value
-    column[4] = along_x
     right_block, left_block = my[:, cols - 128 : cols], my[:, 0:128]
-    weights_r = edge_weights(table, right_block)
-    weights_l = edge_weights(table, left_block)
+    columns = jnp.concatenate(
+        [
+            edge_weights(table, scale_x)[0:4],
+            edge_weights(table, right_block)[0:2],
+            edge_weights(table, left_block)[2:4],
+            jnp.broadcast_to(scale_x, (rows - 8, rows)),
+        ],
+        axis=0,
+    ).T
+    for n in range(9):
+        column[n] = jnp.broadcast_to(columns[:, n : n + 1], (rows, 128))
 
     for side in range(2):
         sx[side] = jnp.zeros((32, cols), F32)
-    metric_row = jnp.broadcast_to(
-        jnp.concatenate([along_x[0:2], along_x[rows - 2 : rows]], axis=0)[:, 0:1], (4, cols)
-    )
-    sx[0, 5:6, :] = metric_row[2:3]
-    sx[0, 13:14, :] = metric_row[3:4]
-    sx[1, 5:6, :] = metric_row[0:1]
-    sx[1, 13:14, :] = metric_row[1:2]
-
-    def place(tile, spot, value):
-        return jnp.where(lane == spot, jnp.broadcast_to(value, tile.shape), tile)
-
-    tile = jnp.zeros((rows, 128), F32)
-    tile = place(tile, 5, right_block[:, 126:127])
-    tile = place(tile, 13, right_block[:, 127:128])
-    tile = place(tile, 37, left_block[:, 0:1])
-    tile = place(tile, 45, left_block[:, 1:2])
-    pack[...] = tile
-
-    wide = [jnp.concatenate([column[n]] * (cols // 128), axis=1) for n in range(4)]
+        sy[side] = jnp.zeros((32, rows), F32)
+    for side, near, block in ((0, rows - 2, right_block), (1, 0, left_block)):
+        for n in range(2):
+            spot = slice(8 * n + 5, 8 * n + 6)
+            sx[side, spot, :] = jnp.broadcast_to(scale_x[:, near + n : near + n + 1], (1, cols))
+            sy[side, spot, :] = jnp.broadcast_to(block[:, near + n : near + n + 1], (1, rows))
+
+    far1, far2 = 32, 64
+
+    def last_face(target, k, here, value, first):
+        over = value[far1:] - value[127:128]
+        target[0, k : k + 1, here] = value[126:127]
+        target[0, 8 + k : 9 + k, here] = value[127:128]
+        target[0, 16 + k : 17 + k, here] = jnp.sum(over * column[first, far1:], axis=0, keepdims=True)
+        over = over[far2 - far1 :]
+        target[0, 24 + k : 25 + k, here] = jnp.sum(over * column[first + 1, far2:], axis=0, keepdims=True)
+
+    def first_face(target, k, here, value, first):
+        over = value[: 128 - far1] - value[0:1]
+        target[1, k : k + 1, here] = value[0:1]
+        target[1, 8 + k : 9 + k, here] = value[1:2]
+        target[1, 16 + k : 17 + k, here] = jnp.sum(over * column[first, : 128 - far1], axis=0, keepdims=True)
+        over = over[: 128 - far2]
+        target[1, 24 + k : 25 + k, here] = jnp.sum(over * column[first + 1, : 128 - far2], axis=0, keepdims=True)
+
     for k in range(fields):
         loads[3 + k].wait()
-        value = f[k]
-        after, before = pltpu.roll(value, rows - 1, 0), pltpu.roll(value, 1, 0)
-        d = after - before
-        e = (after - (value + value)) + before
-        sx[0, k : k + 1, :] = value[rows - 2 : rows - 1]
-        sx[0, 8 + k : 9 + k, :] = value[rows - 1 : rows]
-        sx[1, k : k + 1, :] = value[0:1]
-        sx[1, 8 + k : 9 + k, :] = value[1:2]
-        sx[0, 16 + k : 17 + k, :] = jnp.sum(d * wide[0], axis=0, keepdims=True)
-        sx[1, 16 + k : 17 + k, :] = jnp.sum(d * wide[1], axis=0, keepdims=True)
-        sx[0, 24 + k : 25 + k, :] = jnp.sum(e * wide[2], axis=0, keepdims=True)
-        sx[1, 24 + k : 25 + k, :] = jnp.sum(e * wide[3], axis=0, keepdims=True)
-
-        tile = pack[...]
-        for side in range(2):
-            block = value[:, cols - 128 : cols] if side == 0 else value[:, 0:128]
-            weights = weights_r if side == 0 else weights_l
-            after, before = pltpu.roll(block, 127, 1), pltpu.roll(block, 1, 1)
-            d = after - before
-            e = (after - (block + block)) + before
-            near = 126 if side == 0 else 0
-            tile = place(tile, 32 * side + k, block[:, near : near + 1])
-            tile = place(tile, 32 * side + 8 + k, block[:, near + 1 : near + 2])
-            one = jnp.sum(d * weights[side : side + 1], axis=1, keepdims=True)
-            two = jnp.sum(e * weights[2 + side : 3 + side], axis=1, keepdims=True)
-            tile = place(tile, 32 * side + 16 + k, one)
-            tile = place(tile, 32 * side + 24 + k, two)
-        pack[...] = tile
-
-    turned = pack[...].T
-    sy[0] = turned[0:32]
-    sy[1] = turned[32:64]
-    pl.semaphore_wait(barrier, 4)
+        if k == TABLES:
+            loads[3 + fields].start()
+            loads[4 + fields].start()
+        for c in range(cols // 128):
+            here = slice(128 * c, 128 * c + 128)
+            value = f[k, :, here]
+            last_face(sx, k, here, value, 0)
+            first_face(sx, k, here, value, 2)
+        here = slice(0, rows)
+        last_face(sy, k, here, f[k, :, cols - 128 : cols].T, 4)
+        first_face(sy, k, here, f[k, :, 0:128].T, 6)
+
     copies = []
     for n, peer in enumerate(peers):
         source, target = (sx, hx) if n < 2 else (sy, hy)
-        copy = pltpu.make_async_remote_copy(
-            src_ref=source.at[n % 2],
-            dst_ref=target.at[n % 2],
-            send_sem=send.at[n],
-            recv_sem=recv.at[n],
-            device_id=peer,
-            device_id_type=MESH,
+        copies.append(
+            pltpu.make_async_remote_copy(
+                src_ref=source.at[n % 2],
+                dst_ref=target.at[n % 2],
+                send_sem=send.at[n],
+                recv_sem=recv.at[n],
+                device_id=peer,
+                device_id_type=MESH,
+            )
         )
-        copy.start()
-        copies.append(copy)
-
-    loads[3 + fields].wait()
-    loads[4 + fields].wait()
-    scale_x = jnp.concatenate([column[4]] * (cols // 128), axis=1)
+
+    @pl.when(end)
+    def _():
+        copies[0].start()
+
+    scale_x = jnp.concatenate([column[8]] * (cols // 128), axis=1)
     scale_y = jnp.broadcast_to(my[...], (rows, cols))
 
     def solve(k, carry):
@@ -267,7 +286,46 @@
                 )
         return carry
 
-    lax.fori_loop(0, fields, solve, 0)
+    turn = jnp.where(iy == 0, TURN_FIRST, jnp.where(iy == ny - 1, TURN_LAST, TURN))
+    turn_end = jnp.where(iy == ny - 1, TURN_END - 1, TURN_END)
+
+    def step(k, carry):
+        @pl.when(inner & (k == turn))
+        def _():
+            pl.semaphore_wait(barrier, greeted)
+
+            @pl.when(proxy)
+            def _():
+                pl.semaphore_signal(answer.at[1], inc=1, device_id=right, device_id_type=MESH)
+
+            copies[2].start()
+            copies[3].start()
+            copies[0].start()
+
+            @pl.when(jnp.logical_not(seam))
+            def _():
+                copies[1].start()
+
+        @pl.when(end & (k == turn_end))
+        def _():
+            pl.semaphore_wait(answer.at[1], 1)
+            copies[2].start()
+            copies[3].start()
+            copies[1].start()
+
+        @pl.when(seam & (k == TURN_SEAM))
+        def _():
+            pl.semaphore_wait(answer.at[0], 1)
+            copies[1].start()
+
+        @pl.when(k == 0)
+        def _():
+            loads[3 + fields].wait()
+            loads[4 + fields].wait()
+
+        return solve(k, carry)
+
+    lax.fori_loop(0, fields, step, 0)
     for copy in copies:
         copy.wait()
 
@@ -370,11 +428,11 @@
             pltpu.VMEM((24, 128), F32),
             pltpu.VMEM((2, 2, rows, rows), BF16),
             pltpu.VMEM((2, 2, 512, 256), BF16),
-            pltpu.VMEM((rows, 128), F32),
-            pltpu.VMEM((5, rows, 128), F32),
+            pltpu.VMEM((9, rows, 128), F32),
             pltpu.SemaphoreType.DMA((5 + count,)),
             pltpu.SemaphoreType.DMA((4,)),
             pltpu.SemaphoreType.DMA((4,)),
+            pltpu.SemaphoreType.REGULAR((2,)),
         ],
         compiler_params=pltpu.CompilerParams(collective_id=0, has_side_effects=True, vmem_limit_bytes=20 << 20),
         name="exchange",

time: 16 us -> 15.2 us (0.950)
  the two profiles are of different devices: /device:TPU:8 before, /device:TPU:105 now
where the time goes in v1:
time: 15.2 us; the launch traced here: 15.1 us
  Pallas kernels  14.4 us (95%)
  between operations  0.67 us (4%)
    pallas_call x1, Pallas kernels, on_device(): pl.pallas_call(functools.partial(exchange, lax.axis_size('gx'), lax.axis_...  11.8 us
    pallas_call x1, Pallas kernels, on_device(): pl.pallas_call(join, in_specs=[vmem] * 10, out_specs=[hbm] * 4, out_shape...  2.67 us

profile of v1, /device:TPU:105, one launch (start us, length us, event | category | flops | bytes accessed | tf_op | source)
XLA Modules:
  0.0 15.1 jit_solution(13812749357627004327)
XLA Ops:
  0.6 0.0 copy-start.1
  0.6 0.0 copy-start
  0.7 11.8 %exchange.1 = (f32[5,128,512]{2,1,0:T(8,128)S(1)}, f32[5,128,512]{2,1,0:T(8,128)S(1)}, f32[5,128,512]{2,1,0:T(8,128)S(1)}, f32[5,128,512]{2,1,0:T(8,128)S(1)}, f...) custom-call(f32[5,1,128,512]{3,2,1,0:T(8,128)} %f_hbm.1, ...), custom_call_target="tpu_custom_call" | custom-call | tf_op jit(solution)/shard_map/exchange/pallas_call | solution.py:413
  12.4 0.0 copy-done.1
  12.4 0.0 copy-done
  12.4 2.7 %join.1 = (f32[5,1,128,512]{3,2,1,0:T(8,128)}, f32[5,1,128,512]{3,2,1,0:T(8,128)}, f32[5,1,128,512]{3,2,1,0:T(8,128)}, f32[5,1,128,512]{3,2,1,0:T(8,128)}) custom-call(f32[5,128,512]{2,1,0:T(8,128)S(1)} %get-tuple-element.12.ux1, f32[5,128,512]{2,1,0:T(8,128)S(1)} %get-tuple-element.13.ux2, f32[5,128,512]{2,1,0:T(8,128)S(1)} %get-tuple-element.14.uy1, ...), custom_call_target="tpu_custom_call" | custom-call | tf_op jit(solution)/shard_map/join/pallas_call | solution.py:452
Async XLA Ops:
  0.6 11.8 %copy-start.1 = (bf16[256,512]{1,0:T(8,128)(2,1)S(1)}, bf16[256,512]{1,0:T(8,128)(2,1)}, u32[]{:S(2)}) copy-start(bf16[256,512]{1,0:T(8,128)(2,1)} %constant.14.clone.cy) | copy-start | bytes 786436
  0.6 11.8 %copy-start = (bf16[2,640,128]{2,1,0:T(8,128)(2,1)S(1)}, bf16[2,640,128]{2,1,0:T(8,128)(2,1)}, u32[]{:S(2)}) copy-start(bf16[2,640,128]{2,1,0:T(8,128)(2,1)} %constant.13.clone.cx) | copy-start | bytes 983044

commit v2 on v1

--- a/solution.py
+++ b/solution.py
@@ -11,7 +11,8 @@
 MESH = pl.DeviceIdType.MESH
 F32 = jnp.float32
 BF16 = jnp.bfloat16
-TURN, TURN_FIRST, TURN_LAST, TURN_END, TURN_SEAM = 1, 3, 0, 2, 4
+TURN, TURN_FIRST, TURN_LAST, TURN_END, TURN_SEAM, TURN_PASS = 1, 2, 0, 2, 4, 3
+CHUNKS = 1
 TABLES = 0
 
 ALPHA = (1.0 / 3.0, 2.0 / 11.0)
@@ -152,29 +153,28 @@
     place = lax.rem(ix, run)
     end, proxy, seam = place == run - 1, place == run - 2, place == 0
     inner = jnp.logical_not(end)
+    even = inner & jnp.logical_not(proxy) & (lax.rem(place, 2) == 0)
+    odd = inner & (lax.rem(place, 2) == 1)
+    first, last = iy == 0, iy == ny - 1
+    spared = even & first
     right, left, up, down = peers
     barrier = pltpu.get_barrier_semaphore()
 
-    def greet(peer):
-        pl.semaphore_signal(barrier, inc=1, device_id=peer, device_id_type=MESH)
-
-    greet(left)
-
-    @pl.when(inner)
-    def _():
-        greet(up)
-        greet(down)
-
-    @pl.when(jnp.logical_not(end | proxy))
-    def _():
-        greet(right)
-
-    @pl.when(end)
-    def _():
-        greet({**left, **up})
-        greet({**left, **down})
-
-    greeted = jnp.where(end, 1, jnp.where(proxy, 6, jnp.where(seam, 3, 4)))
+    def greet(when, *sides):
+        @pl.when(when)
+        def _():
+            peer = {k: v for side in sides for k, v in side.items()}
+            pl.semaphore_signal(barrier, inc=1, device_id=peer, device_id_type=MESH)
+
+    greet(ix >= 0, left)
+    greet(jnp.logical_not(end | proxy), right)
+    greet(inner & jnp.logical_not(even & last), up)
+    greet(even & last, right, up)
+    greet(inner, down)
+    greet(end, left, up)
+    greet(end, left, down)
+    greeted = jnp.where(end, 1, jnp.where(proxy, 6, 4 - seam.astype(jnp.int32)))
+    greeted = greeted - spared.astype(jnp.int32) + (odd & first).astype(jnp.int32)
     loads = [
         pltpu.make_async_copy(mx_hbm, mx, load.at[0]),
         pltpu.make_async_copy(my_hbm, my, load.at[1]),
@@ -244,27 +244,35 @@
             value = f[k, :, here]
             last_face(sx, k, here, value, 0)
             first_face(sx, k, here, value, 2)
+
+    copies = []
+    for n, peer in enumerate(peers):
+        source, target, parts = (sx, hx, CHUNKS) if n < 2 else (sy, hy, 1)
+        width = source.shape[2] // parts
+        copies.append(
+            [
+                pltpu.make_async_remote_copy(
+                    src_ref=source.at[n % 2, :, width * c : width * c + width],
+                    dst_ref=target.at[n % 2, :, width * c : width * c + width],
+                    send_sem=send.at[n, c],
+                    recv_sem=recv.at[n, c],
+                    device_id=peer,
+                    device_id_type=MESH,
+                )
+                for c in range(parts)
+            ]
+        )
+
+    @pl.when(end)
+    def _():
+        for copy in copies[0]:
+            copy.start()
+
+    for k in range(fields):
         here = slice(0, rows)
         last_face(sy, k, here, f[k, :, cols - 128 : cols].T, 4)
         first_face(sy, k, here, f[k, :, 0:128].T, 6)
 
-    copies = []
-    for n, peer in enumerate(peers):
-        source, target = (sx, hx) if n < 2 else (sy, hy)
-        copies.append(
-            pltpu.make_async_remote_copy(
-                src_ref=source.at[n % 2],
-                dst_ref=target.at[n % 2],
-                send_sem=send.at[n],
-                recv_sem=recv.at[n],
-                device_id=peer,
-                device_id_type=MESH,
-            )
-        )
-
-    @pl.when(end)
-    def _():
-        copies[0].start()
 
     scale_x = jnp.concatenate([column[8]] * (cols // 128), axis=1)
     scale_y = jnp.broadcast_to(my[...], (rows, cols))
@@ -286,8 +294,13 @@
                 )
         return carry
 
-    turn = jnp.where(iy == 0, TURN_FIRST, jnp.where(iy == ny - 1, TURN_LAST, TURN))
-    turn_end = jnp.where(iy == ny - 1, TURN_END - 1, TURN_END)
+    heard_late = first & (odd | proxy)
+    turn = jnp.where(heard_late, TURN_FIRST, jnp.where(last, TURN_LAST, TURN))
+    turn_end = jnp.where(first, TURN_PASS, jnp.where(last, TURN_END - 1, TURN_END))
+
+    def send_x(n):
+        for copy in copies[n]:
+            copy.start()
 
     def step(k, carry):
         @pl.when(inner & (k == turn))
@@ -298,25 +311,38 @@
             def _():
                 pl.semaphore_signal(answer.at[1], inc=1, device_id=right, device_id_type=MESH)
 
-            copies[2].start()
-            copies[3].start()
-            copies[0].start()
+            @pl.when(odd & first)
+            def _():
+                pl.semaphore_signal(answer.at[1], inc=1, device_id=left, device_id_type=MESH)
+
+            copies[2][0].start()
+
+            @pl.when(jnp.logical_not(spared))
+            def _():
+                copies[3][0].start()
+
+            send_x(0)
 
             @pl.when(jnp.logical_not(seam))
             def _():
-                copies[1].start()
+                send_x(1)
 
         @pl.when(end & (k == turn_end))
         def _():
             pl.semaphore_wait(answer.at[1], 1)
-            copies[2].start()
-            copies[3].start()
-            copies[1].start()
+            copies[2][0].start()
+            copies[3][0].start()
+            send_x(1)
+
+        @pl.when(spared & (k == TURN_PASS))
+        def _():
+            pl.semaphore_wait(answer.at[1], 1)
+            copies[3][0].start()
 
         @pl.when(seam & (k == TURN_SEAM))
         def _():
             pl.semaphore_wait(answer.at[0], 1)
-            copies[1].start()
+            send_x(1)
 
         @pl.when(k == 0)
         def _():
@@ -326,8 +352,9 @@
         return solve(k, carry)
 
     lax.fori_loop(0, fields, step, 0)
-    for copy in copies:
-        copy.wait()
+    for group in copies:
+        for copy in group:
+            copy.wait()
 
 
 def face_values(own, far, side):
@@ -430,8 +457,8 @@
             pltpu.VMEM((2, 2, 512, 256), BF16),
             pltpu.VMEM((9, rows, 128), F32),
             pltpu.SemaphoreType.DMA((5 + count,)),
-            pltpu.SemaphoreType.DMA((4,)),
-            pltpu.SemaphoreType.DMA((4,)),
+            pltpu.SemaphoreType.DMA((4, CHUNKS)),
+            pltpu.SemaphoreType.DMA((4, CHUNKS)),
             pltpu.SemaphoreType.REGULAR((2,)),
         ],
         compiler_params=pltpu.CompilerParams(collective_id=0, has_side_effects=True, vmem_limit_bytes=20 << 20),

time: 15.2 us -> 13.8 us (0.908)
  the two profiles are of different devices: /device:TPU:105 before, /device:TPU:6 now
where the time goes in v2:
time: 13.8 us; the launch traced here: 13.7 us
  Pallas kernels  13 us (94%)
  between operations  0.67 us (5%)
    pallas_call x1, Pallas kernels, on_device(): pl.pallas_call(functools.partial(exchange, lax.axis_size('gx'), lax.axis_...  10.4 us
    pallas_call x1, Pallas kernels, on_device(): pl.pallas_call(join, in_specs=[vmem] * 10, out_specs=[hbm] * 4, out_shape...  2.67 us

profile of v2, /device:TPU:6, one launch (start us, length us, event | category | flops | bytes accessed | tf_op | source)
XLA Modules:
  0.0 13.7 jit_solution(8011899702205153169)
XLA Ops:
  0.6 0.0 copy-start.1
  0.6 0.0 copy-start
  0.7 10.4 %exchange.1 = (f32[5,128,512]{2,1,0:T(8,128)S(1)}, f32[5,128,512]{2,1,0:T(8,128)S(1)}, f32[5,128,512]{2,1,0:T(8,128)S(1)}, f32[5,128,512]{2,1,0:T(8,128)S(1)}, f...) custom-call(f32[5,1,128,512]{3,2,1,0:T(8,128)} %f_hbm.1, ...), custom_call_target="tpu_custom_call" | custom-call | tf_op jit(solution)/shard_map/exchange/pallas_call | solution.py:440
  11.0 0.0 copy-done.1
  11.0 0.0 copy-done
  11.1 2.7 %join.1 = (f32[5,1,128,512]{3,2,1,0:T(8,128)}, f32[5,1,128,512]{3,2,1,0:T(8,128)}, f32[5,1,128,512]{3,2,1,0:T(8,128)}, f32[5,1,128,512]{3,2,1,0:T(8,128)}) custom-call(f32[5,128,512]{2,1,0:T(8,128)S(1)} %get-tuple-element.12.ux1, f32[5,128,512]{2,1,0:T(8,128)S(1)} %get-tuple-element.13.ux2, f32[5,128,512]{2,1,0:T(8,128)S(1)} %get-tuple-element.14.uy1, ...), custom_call_target="tpu_custom_call" | custom-call | tf_op jit(solution)/shard_map/join/pallas_call | solution.py:479
Async XLA Ops:
  0.6 10.4 %copy-start.1 = (bf16[256,512]{1,0:T(8,128)(2,1)S(1)}, bf16[256,512]{1,0:T(8,128)(2,1)}, u32[]{:S(2)}) copy-start(bf16[256,512]{1,0:T(8,128)(2,1)} %constant.14.clone.cy) | copy-start | bytes 786436
  0.6 10.4 %copy-start = (bf16[2,640,128]{2,1,0:T(8,128)(2,1)S(1)}, bf16[2,640,128]{2,1,0:T(8,128)(2,1)}, u32[]{:S(2)}) copy-start(bf16[2,640,128]{2,1,0:T(8,128)(2,1)} %constant.13.clone.cx) | copy-start | bytes 983044

commit v3 on v2

--- a/solution.py
+++ b/solution.py
@@ -11,8 +11,9 @@
 MESH = pl.DeviceIdType.MESH
 F32 = jnp.float32
 BF16 = jnp.bfloat16
-TURN, TURN_FIRST, TURN_LAST, TURN_END, TURN_SEAM, TURN_PASS = 1, 2, 0, 2, 4, 3
+TURN, TURN_FIRST, TURN_LAST, TURN_END, TURN_SEAM, TURN_PASS = 1, 3, 0, 2, 3, 3
 CHUNKS = 1
+SPARE = (6, 7, 14, 15, 21)
 TABLES = 0
 
 ALPHA = (1.0 / 3.0, 2.0 / 11.0)
@@ -41,7 +42,7 @@
 def line_tables(count):
     cells = np.arange(count)
     out = [halves(green(cells[:, None] - cells[None, :], w)) for w in range(2)]
-    return np.stack([np.stack(pair) for pair in out])
+    return np.stack([np.concatenate([high, high, low], axis=1) for high, low in out])
 
 
 def window_tables():
@@ -208,8 +209,8 @@
         column[n] = jnp.broadcast_to(columns[:, n : n + 1], (rows, 128))
 
     for side in range(2):
-        sx[side] = jnp.zeros((32, cols), F32)
-        sy[side] = jnp.zeros((32, rows), F32)
+        sx[side] = jnp.zeros((24, cols), F32)
+        sy[side] = jnp.zeros((24, rows), F32)
     for side, near, block in ((0, rows - 2, right_block), (1, 0, left_block)):
         for n in range(2):
             spot = slice(8 * n + 5, 8 * n + 6)
@@ -224,7 +225,7 @@
         target[0, 8 + k : 9 + k, here] = value[127:128]
         target[0, 16 + k : 17 + k, here] = jnp.sum(over * column[first, far1:], axis=0, keepdims=True)
         over = over[far2 - far1 :]
-        target[0, 24 + k : 25 + k, here] = jnp.sum(over * column[first + 1, far2:], axis=0, keepdims=True)
+        target[0, SPARE[k] : SPARE[k] + 1, here] = jnp.sum(over * column[first + 1, far2:], axis=0, keepdims=True)
 
     def first_face(target, k, here, value, first):
         over = value[: 128 - far1] - value[0:1]
@@ -232,7 +233,7 @@
         target[1, 8 + k : 9 + k, here] = value[1:2]
         target[1, 16 + k : 17 + k, here] = jnp.sum(over * column[first, : 128 - far1], axis=0, keepdims=True)
         over = over[: 128 - far2]
-        target[1, 24 + k : 25 + k, here] = jnp.sum(over * column[first + 1, : 128 - far2], axis=0, keepdims=True)
+        target[1, SPARE[k] : SPARE[k] + 1, here] = jnp.sum(over * column[first + 1, : 128 - far2], axis=0, keepdims=True)
 
     for k in range(fields):
         loads[3 + k].wait()
@@ -243,7 +244,6 @@
             here = slice(128 * c, 128 * c + 128)
             value = f[k, :, here]
             last_face(sx, k, here, value, 0)
-            first_face(sx, k, here, value, 2)
 
     copies = []
     for n, peer in enumerate(peers):
@@ -269,6 +269,9 @@
             copy.start()
 
     for k in range(fields):
+        for c in range(cols // 128):
+            here = slice(128 * c, 128 * c + 128)
+            first_face(sx, k, here, f[k, :, here], 2)
         here = slice(0, rows)
         last_face(sy, k, here, f[k, :, cols - 128 : cols].T, 4)
         first_face(sy, k, here, f[k, :, 0:128].T, 6)
@@ -281,7 +284,7 @@
         value = f[k]
         for which, (right, out) in enumerate(zip(right_sides(value, scale_x, 0), (ux1, ux2))):
             high, low = split(right)
-            out[k] = dot(tx[which, 0], high) + dot(tx[which, 0], low) + dot(tx[which, 1], high)
+            out[k] = dot(tx[which], jnp.concatenate([high, low, high], axis=0))
         for which, (right, out) in enumerate(zip(right_sides(value, scale_y, 1), (uy1, uy2))):
             high, low = split(right)
             for half in range(2):
@@ -296,7 +299,7 @@
 
     heard_late = first & (odd | proxy)
     turn = jnp.where(heard_late, TURN_FIRST, jnp.where(last, TURN_LAST, TURN))
-    turn_end = jnp.where(first, TURN_PASS, jnp.where(last, TURN_END - 1, TURN_END))
+    turn_end = jnp.where(first, TURN_PASS + 1, jnp.where(last, TURN_LAST, TURN_END))
 
     def send_x(n):
         for copy in copies[n]:
@@ -379,7 +382,10 @@
             if which == 0
             else (metric0 * metric0, metric1 * metric1, beyond1 * beyond1, beyond2 * beyond2)
         )
-        carry = there[16 + 8 * which : 24 + 8 * which]
+        carry = there[16:24]
+        if which == 1:
+            spare = [there[row : row + 1] for row in SPARE]
+            carry = jnp.concatenate([*spare, jnp.zeros((3, there.shape[1]), F32)], axis=0)
         carry = carry + gain * (rho * far_by * (b2 * over) + b1 * (near_by * over + far_by * here))
         zero = m0 * (near_by * here + far_by * over)
         one = (far_by * m1) * here
@@ -443,17 +449,17 @@
         out_specs=[vmem] * 8,
         out_shape=[
             *[block] * 4,
-            pltpu.VMEM((2, 32, cols), F32),
-            pltpu.VMEM((2, 32, rows), F32),
-            pltpu.VMEM((2, 32, cols), F32),
-            pltpu.VMEM((2, 32, rows), F32),
+            pltpu.VMEM((2, 24, cols), F32),
+            pltpu.VMEM((2, 24, rows), F32),
+            pltpu.VMEM((2, 24, cols), F32),
+            pltpu.VMEM((2, 24, rows), F32),
         ],
         scratch_shapes=[
             pltpu.VMEM((count, rows, cols), F32),
             pltpu.VMEM((1, rows), F32),
             pltpu.VMEM((1, cols), F32),
             pltpu.VMEM((24, 128), F32),
-            pltpu.VMEM((2, 2, rows, rows), BF16),
+            pltpu.VMEM((2, rows, 3 * rows), BF16),
             pltpu.VMEM((2, 2, 512, 256), BF16),
             pltpu.VMEM((9, rows, 128), F32),
             pltpu.SemaphoreType.DMA((5 + count,)),

time: 13.8 us -> 13.6 us (0.986)
  Pallas kernels: 13 us -> 12.8 us
    pallas_call x1, Pallas kernels: 10.4 us -> 10.1 us  [on_device(): pl.pallas_call(functools.partial(exchange, lax.axis_size('gx'), lax.axis_...]
where the time goes in v3:
time: 13.6 us; the launch traced here: 13.5 us
  Pallas kernels  12.8 us (94%)
  between operations  0.67 us (5%)
    pallas_call x1, Pallas kernels, on_device(): pl.pallas_call(functools.partial(exchange, lax.axis_size('gx'), lax.axis_...  10.1 us
    pallas_call x1, Pallas kernels, on_device(): pl.pallas_call(join, in_specs=[vmem] * 10, out_specs=[hbm] * 4, out_shape...  2.68 us

profile of v3, /device:TPU:6, one launch (start us, length us, event | category | flops | bytes accessed | tf_op | source)
XLA Modules:
  0.0 13.5 jit_solution(10354537760932897674)
XLA Ops:
  0.6 0.0 copy-start.1
  0.6 0.0 copy-start
  0.7 10.1 %exchange.1 = (f32[5,128,512]{2,1,0:T(8,128)S(1)}, f32[5,128,512]{2,1,0:T(8,128)S(1)}, f32[5,128,512]{2,1,0:T(8,128)S(1)}, f32[5,128,512]{2,1,0:T(8,128)S(1)}, f...) custom-call(f32[5,1,128,512]{3,2,1,0:T(8,128)} %f_hbm.1, ...), custom_call_target="tpu_custom_call" | custom-call | tf_op jit(solution)/shard_map/exchange/pallas_call | solution.py:446
  10.8 0.0 copy-done.1
  10.8 0.0 copy-done
  10.8 2.7 %join.1 = (f32[5,1,128,512]{3,2,1,0:T(8,128)}, f32[5,1,128,512]{3,2,1,0:T(8,128)}, f32[5,1,128,512]{3,2,1,0:T(8,128)}, f32[5,1,128,512]{3,2,1,0:T(8,128)}) custom-call(f32[5,128,512]{2,1,0:T(8,128)S(1)} %get-tuple-element.12.ux1, f32[5,128,512]{2,1,0:T(8,128)S(1)} %get-tuple-element.13.ux2, f32[5,128,512]{2,1,0:T(8,128)S(1)} %get-tuple-element.14.uy1, ...), custom_call_target="tpu_custom_call" | custom-call | tf_op jit(solution)/shard_map/join/pallas_call | solution.py:485
Async XLA Ops:
  0.6 10.1 %copy-start.1 = (bf16[256,512]{1,0:T(8,128)(2,1)S(1)}, bf16[256,512]{1,0:T(8,128)(2,1)}, u32[]{:S(2)}) copy-start(bf16[256,512]{1,0:T(8,128)(2,1)} %constant.14.clone.cy) | copy-start | bytes 786436
  0.6 10.1 %copy-start = (bf16[2,640,128]{2,1,0:T(8,128)(2,1)S(1)}, bf16[2,640,128]{2,1,0:T(8,128)(2,1)}, u32[]{:S(2)}) copy-start(bf16[2,640,128]{2,1,0:T(8,128)(2,1)} %constant.13.clone.cx) | copy-start | bytes 983044

commit v4 on v3

--- a/solution.py
+++ b/solution.py
@@ -399,16 +399,13 @@
 ):
     fields, rows, cols = ux1.shape
     middle = slice(128, cols - 128)
-    copies = []
-
-    def put(source, target):
-        copy = pltpu.make_async_copy(source, target, done.at[len(copies)])
-        copy.start()
-        copies.append(copy)
-
-    for part, out in ((uy1, oy1), (uy2, oy2)):
+
+    def put(source, target, n):
+        pltpu.make_async_copy(source, target, done.at[n]).start()
+
+    for n, (part, out) in enumerate(((uy1, oy1), (uy2, oy2))):
         for k in range(fields):
-            put(part.at[k, :, middle], out.at[k, 0, :, middle])
+            put(part.at[k, :, middle], out.at[k, 0, :, middle], 2 + n)
 
     own, far = (sx[0], sx[1]), (hx[0], hx[1])
     left, right = face_values(own, far, 0), face_values(own, far, 1)
@@ -418,7 +415,7 @@
         for k in range(fields):
             lhs = cx[which, rows * k : rows * (k + 1), 0:96]
             stage_x[which, k] = part[k] + dot(lhs, stack)
-            put(stage_x.at[which, k], out.at[k, 0])
+            put(stage_x.at[which, k], out.at[k, 0], which)
 
     own, far = (sy[0], sy[1]), (hy[0], hy[1])
     left, right = face_values(own, far, 0), face_values(own, far, 1)
@@ -433,9 +430,9 @@
                 place = slice(0, 128) if side == 0 else slice(cols - 128, cols)
                 n = 2 * which + side
                 stage_y[n, k] = part[k, :, place] + both[:, 128 * n : 128 * n + 128]
-                put(stage_y.at[n, k], out.at[k, 0, :, place])
-    for copy in copies:
-        copy.wait()
+                put(stage_y.at[n, k], out.at[k, 0, :, place], 2 + which)
+    for n, (part, out) in enumerate(((ux1, ox1), (ux2, ox2), (uy1, oy1), (uy2, oy2))):
+        pltpu.make_async_copy(part, out.at[:, 0], done.at[n]).wait()
 
 
 def on_device(fields, metric_x, metric_y):
@@ -490,7 +487,7 @@
         scratch_shapes=[
             pltpu.VMEM((2, count, rows, cols), F32),
             pltpu.VMEM((4, count, rows, 128), F32),
-            pltpu.SemaphoreType.DMA((8 * count,)),
+            pltpu.SemaphoreType.DMA((4,)),
         ],
         compiler_params=pltpu.CompilerParams(vmem_limit_bytes=20 << 20),
         name="join",

time: 13.6 us -> 13.3 us (0.978)
  Pallas kernels: 12.8 us -> 12.5 us
    pallas_call x1, Pallas kernels: 2.68 us -> 2.35 us  [on_device(): pl.pallas_call(join, in_specs=[vmem] * 10, out_specs=[hbm] * 4, out_shape...]
where the time goes in v4:
time: 13.3 us; the launch traced here: 13.2 us
  Pallas kernels  12.5 us (94%)
  between operations  0.67 us (5%)
    pallas_call x1, Pallas kernels, on_device(): pl.pallas_call(functools.partial(exchange, lax.axis_size('gx'), lax.axis_...  10.1 us
    pallas_call x1, Pallas kernels, on_device(): pl.pallas_call(join, in_specs=[vmem] * 10, out_specs=[hbm] * 4, out_shape...  2.35 us

profile of v4, /device:TPU:6, one launch (start us, length us, event | category | flops | bytes accessed | tf_op | source)
XLA Modules:
  0.0 13.2 jit_solution(6820823613345513400)
XLA Ops:
  0.6 0.0 copy-start.1
  0.6 0.0 copy-start
  0.7 10.1 %exchange.1 = (f32[5,128,512]{2,1,0:T(8,128)S(1)}, f32[5,128,512]{2,1,0:T(8,128)S(1)}, f32[5,128,512]{2,1,0:T(8,128)S(1)}, f32[5,128,512]{2,1,0:T(8,128)S(1)}, f...) custom-call(f32[5,1,128,512]{3,2,1,0:T(8,128)} %f_hbm.1, ...), custom_call_target="tpu_custom_call" | custom-call | tf_op jit(solution)/shard_map/exchange/pallas_call | solution.py:443
  10.8 0.0 copy-done.1
  10.8 0.0 copy-done
  10.8 2.4 %join.1 = (f32[5,1,128,512]{3,2,1,0:T(8,128)}, f32[5,1,128,512]{3,2,1,0:T(8,128)}, f32[5,1,128,512]{3,2,1,0:T(8,128)}, f32[5,1,128,512]{3,2,1,0:T(8,128)}) custom-call(f32[5,128,512]{2,1,0:T(8,128)S(1)} %get-tuple-element.12.ux1, f32[5,128,512]{2,1,0:T(8,128)S(1)} %get-tuple-element.13.ux2, f32[5,128,512]{2,1,0:T(8,128)S(1)} %get-tuple-element.14.uy1, ...), custom_call_target="tpu_custom_call" | custom-call | tf_op jit(solution)/shard_map/join/pallas_call | solution.py:482
Async XLA Ops:
  0.6 10.1 %copy-start.1 = (bf16[256,512]{1,0:T(8,128)(2,1)S(1)}, bf16[256,512]{1,0:T(8,128)(2,1)}, u32[]{:S(2)}) copy-start(bf16[256,512]{1,0:T(8,128)(2,1)} %constant.14.clone.cy) | copy-start | bytes 786436
  0.6 10.1 %copy-start = (bf16[2,640,128]{2,1,0:T(8,128)(2,1)S(1)}, bf16[2,640,128]{2,1,0:T(8,128)(2,1)}, u32[]{:S(2)}) copy-start(bf16[2,640,128]{2,1,0:T(8,128)(2,1)} %constant.13.clone.cx) | copy-start | bytes 983044

commit v5 on v4

--- a/solution.py
+++ b/solution.py
@@ -143,6 +143,16 @@
     f, mx, my, edge, tx, ty, column, load, send, recv, answer,
 ):
     fields, rows, cols = f.shape
+    loads = [
+        pltpu.make_async_copy(mx_hbm, mx, load.at[0]),
+        pltpu.make_async_copy(my_hbm, my, load.at[1]),
+        pltpu.make_async_copy(edge_hbm, edge, load.at[2]),
+    ]
+    loads += [pltpu.make_async_copy(f_hbm.at[k, 0], f.at[k], load.at[5 + k]) for k in range(fields)]
+    loads += [pltpu.make_async_copy(tx_hbm, tx, load.at[3]), pltpu.make_async_copy(ty_hbm, ty, load.at[4])]
+    for copy in loads[: 3 + fields]:
+        copy.start()
+
     ix, iy = lax.axis_index("gx"), lax.axis_index("gy")
     peers = (
         {"gx": lax.rem(ix + 1, nx)},
@@ -176,16 +186,6 @@
     greet(end, left, down)
     greeted = jnp.where(end, 1, jnp.where(proxy, 6, 4 - seam.astype(jnp.int32)))
     greeted = greeted - spared.astype(jnp.int32) + (odd & first).astype(jnp.int32)
-    loads = [
-        pltpu.make_async_copy(mx_hbm, mx, load.at[0]),
-        pltpu.make_async_copy(my_hbm, my, load.at[1]),
-        pltpu.make_async_copy(edge_hbm, edge, load.at[2]),
-    ]
-    loads += [pltpu.make_async_copy(f_hbm.at[k, 0], f.at[k], load.at[5 + k]) for k in range(fields)]
-    loads += [pltpu.make_async_copy(tx_hbm, tx, load.at[3]), pltpu.make_async_copy(ty_hbm, ty, load.at[4])]
-    for copy in loads[: 3 + fields]:
-        copy.start()
-
     @pl.when(end)
     def _():
         pl.semaphore_wait(barrier, greeted)

time: 13.3 us -> 13.2 us (level)
  no operation moved by 1% of the time
where the time goes in v5:
time: 13.2 us; the launch traced here: 13.1 us
  Pallas kernels  12.4 us (94%)
  between operations  0.67 us (5%)
    pallas_call x1, Pallas kernels, on_device(): pl.pallas_call(functools.partial(exchange, lax.axis_size('gx'), lax.axis_...  10.1 us
    pallas_call x1, Pallas kernels, on_device(): pl.pallas_call(join, in_specs=[vmem] * 10, out_specs=[hbm] * 4, out_shape...  2.35 us

profile of v5, /device:TPU:6, one launch (start us, length us, event | category | flops | bytes accessed | tf_op | source)
XLA Modules:
  0.0 13.1 jit_solution(17200713107797313985)
XLA Ops:
  0.6 0.0 copy-start.1
  0.6 0.0 copy-start
  0.7 10.1 %exchange.1 = (f32[5,128,512]{2,1,0:T(8,128)S(1)}, f32[5,128,512]{2,1,0:T(8,128)S(1)}, f32[5,128,512]{2,1,0:T(8,128)S(1)}, f32[5,128,512]{2,1,0:T(8,128)S(1)}, f...) custom-call(f32[5,1,128,512]{3,2,1,0:T(8,128)} %f_hbm.1, ...), custom_call_target="tpu_custom_call" | custom-call | tf_op jit(solution)/shard_map/exchange/pallas_call | solution.py:443
  10.7 0.0 copy-done.1
  10.8 0.0 copy-done
  10.8 2.4 %join.1 = (f32[5,1,128,512]{3,2,1,0:T(8,128)}, f32[5,1,128,512]{3,2,1,0:T(8,128)}, f32[5,1,128,512]{3,2,1,0:T(8,128)}, f32[5,1,128,512]{3,2,1,0:T(8,128)}) custom-call(f32[5,128,512]{2,1,0:T(8,128)S(1)} %get-tuple-element.12.ux1, f32[5,128,512]{2,1,0:T(8,128)S(1)} %get-tuple-element.13.ux2, f32[5,128,512]{2,1,0:T(8,128)S(1)} %get-tuple-element.14.uy1, ...), custom_call_target="tpu_custom_call" | custom-call | tf_op jit(solution)/shard_map/join/pallas_call | solution.py:482
Async XLA Ops:
  0.6 10.1 %copy-start.1 = (bf16[256,512]{1,0:T(8,128)(2,1)S(1)}, bf16[256,512]{1,0:T(8,128)(2,1)}, u32[]{:S(2)}) copy-start(bf16[256,512]{1,0:T(8,128)(2,1)} %constant.14.clone.cy) | copy-start | bytes 786436
  0.6 10.1 %copy-start = (bf16[2,640,128]{2,1,0:T(8,128)(2,1)S(1)}, bf16[2,640,128]{2,1,0:T(8,128)(2,1)}, u32[]{:S(2)}) copy-start(bf16[2,640,128]{2,1,0:T(8,128)(2,1)} %constant.13.clone.cx) | copy-start | bytes 983044
